TPU v7x, 128 devices: a whole 4x4x4 slice. The times are simulated.
128 devices in a mesh: member: 2 (over y_hi), gridy: 8 (over x, core), gridx: 8 (over z, y_lo).
Axes of the slice: x: 4, y: 4 (y_hi: 2, y_lo: 2; y = y_hi * 2 + y_lo), z: 4, core: 2. Of those that a mesh axis runs over, the one named last changes fastest.
Arguments:
- temp: float32 [4, 4, 512, 2048], P('member', None, 'gridy', 'gridx'), may hold values from -6 to 6
- salt: float32 [4, 4, 512, 2048], P('member', None, 'gridy', 'gridx'), may hold values from -6 to 6
- uvel: float32 [4, 4, 512, 2048], P('member', None, 'gridy', 'gridx'), may hold values from -3 to 3
- vvel: float32 [4, 4, 512, 2048], P('member', None, 'gridy', 'gridx'), may hold values from -3 to 3
- eta: float32 [4, 512, 2048], P('member', 'gridy', 'gridx'), may hold values from -6 to 6
- land_mask: int32 [512, 2048], P('gridy', 'gridx'), may hold values 0 or 1
- clone_source: int32 [4], P('member'), may hold values from 0 to 3
Outputs:
- new_temp: float32 [4, 4, 512, 2048], P('member', None, 'gridy', 'gridx')
- new_salt: float32 [4, 4, 512, 2048], P('member', None, 'gridy', 'gridx')
- new_uvel: float32 [4, 4, 512, 2048], P('member', None, 'gridy', 'gridx')
- new_vvel: float32 [4, 4, 512, 2048], P('member', None, 'gridy', 'gridx')
- new_eta: float32 [4, 512, 2048], P('member', 'gridy', 'gridx')
- overturning: float32 [4, 4, 512], P('member', None, 'gridy')
- clone_weight: float32 [4], P('member')
All inputs are finite; a program needn't handle non-finite values. No bound on the sum of `land_mask` on one device may be relied on, other than what follows from the above.
Results may differ from a plain program's by a relative error of at most 0.0001.
Values sent between devices are 32-bit elements; how exact they have to be, the bound alone decides.
A program may use at most 128 MiB of HBM per device.

v0:
```python
import jax
import jax.numpy as jnp
from jax import lax
from jax.sharding import PartitionSpec as P

STEPS = 2
ITERS = 3


ALPHA_T = 0.8
BETA_S = 0.6
PRESS_K = 0.25
STEP_DT = 0.1
KAPPA = 0.1
VISCOSITY = 0.1
DRAG_K = 0.05
CORI_K = 1.0
SURF_C = 4.0
DIV_K = 0.5
GRAV_K = 0.5


def padded_2(block, sides, width):
    for axis, dim in sides:
        count = lax.axis_size(axis)
        forward = [(i, i + 1) for i in range(count - 1)]
        forward.append((count - 1, 0))
        backward = [(target, source) for source, target in forward]
        low = lax.ppermute(
            lax.slice_in_dim(block, block.shape[dim] - width, None, axis=dim), axis, forward
        )
        high = lax.ppermute(lax.slice_in_dim(block, 0, width, axis=dim), axis, backward)
        block = jnp.concatenate([low, block, high], axis=dim)
    return block


def pressure(temp, salt):
    return PRESS_K * jnp.cumsum(BETA_S * salt - ALPHA_T * temp, axis=-3)


def split_rims(padded, south_keep, north_keep):
    east_side = padded[..., 1:-1, 2:]
    west_side = padded[..., 1:-1, :-2]
    north_side = padded[..., 2:, 1:-1]
    south_side = padded[..., :-2, 1:-1]
    north_side = north_side.at[..., -1, :].multiply(north_keep)
    south_side = south_side.at[..., 0, :].multiply(south_keep)
    return (east_side, west_side, north_side, south_side)


def volume_sides(fields, south_keep, north_keep):
    padded = padded_2(jnp.stack(fields), (("gridy", 3), ("gridx", 4)), 1)
    return split_rims(padded, south_keep, north_keep)


def surface_sides(fields, south_keep, north_keep):
    padded = padded_2(jnp.stack(fields), (("gridy", 2), ("gridx", 3)), 1)
    return split_rims(padded, south_keep, north_keep)


def surface_apply(field, south_keep, north_keep):
    east_side, west_side, north_side, south_side = surface_sides((field,), south_keep, north_keep)
    return (1.0 + 4.0 * SURF_C) * field - SURF_C * (
        east_side[0] + west_side[0] + north_side[0] + south_side[0]
    )


def member_total(values):
    return jnp.sum(values, axis=(1, 2))


def squared_norm(residual):
    return lax.psum(member_total(residual * residual), ("gridy", "gridx"))


def widen(values):
    return values[:, None, None]


def surface_solve(rhs, south_keep, north_keep):
    solution = jnp.zeros_like(rhs)
    residual = rhs
    direction = rhs
    norm_now = squared_norm(residual)
    for count in range(ITERS):
        image = surface_apply(direction, south_keep, north_keep)
        alpha = norm_now / lax.psum(member_total(direction * image), ("gridy", "gridx"))
        solution = solution + widen(alpha) * direction
        residual = residual - widen(alpha) * image
        norm_next = squared_norm(residual)
        direction = residual + widen(norm_next / norm_now) * direction
        norm_now = norm_next
    return solution


def shards(temp, salt, uvel, vvel, eta, land_mask, clone_source):
    levels = temp.shape[1]
    rows = temp.shape[2]
    cols = temp.shape[3]
    ocean = land_mask.astype(jnp.float32)
    tile_row = lax.axis_index("gridy")
    tile_count = lax.axis_size("gridy")
    total_rows = rows * tile_count
    total_cols = cols * lax.axis_size("gridx")
    south_keep = (tile_row > 0).astype(jnp.float32)
    north_keep = (tile_row < tile_count - 1).astype(jnp.float32)
    latitude = (tile_row * rows + jnp.arange(rows, dtype=jnp.int32)).astype(jnp.float32) + 0.5
    coriolis = (CORI_K * (2.0 * latitude / total_rows - 1.0))[:, None]
    for count in range(STEPS):
        press = pressure(temp, salt)
        east_side, west_side, north_side, south_side = volume_sides(
            (temp, salt, uvel, vvel, press), south_keep, north_keep
        )
        lap_temp = east_side[0] + west_side[0] + north_side[0] + south_side[0] - 4.0 * temp
        lap_salt = east_side[1] + west_side[1] + north_side[1] + south_side[1] - 4.0 * salt
        lap_uvel = east_side[2] + west_side[2] + north_side[2] + south_side[2] - 4.0 * uvel
        lap_vvel = east_side[3] + west_side[3] + north_side[3] + south_side[3] - 4.0 * vvel
        temp_next = ocean * (
            temp
            - STEP_DT
            * 0.5
            * (uvel * (east_side[0] - west_side[0]) + vvel * (north_side[0] - south_side[0]))
            + KAPPA * lap_temp
        )
        salt_next = ocean * (
            salt
            - STEP_DT
            * 0.5
            * (uvel * (east_side[1] - west_side[1]) + vvel * (north_side[1] - south_side[1]))
            + KAPPA * lap_salt
        )
        ustar = ocean * (
            uvel
            + STEP_DT * (coriolis * vvel - 0.5 * (east_side[4] - west_side[4]) - DRAG_K * uvel)
            + VISCOSITY * lap_uvel
        )
        vstar = ocean * (
            vvel
            + STEP_DT * (-coriolis * uvel - 0.5 * (north_side[4] - south_side[4]) - DRAG_K * vvel)
            + VISCOSITY * lap_vvel
        )
        trans_u = jnp.sum(ustar, axis=1)
        trans_v = jnp.sum(vstar, axis=1)
        east_t, west_t, north_t, south_t = surface_sides((trans_u, trans_v), south_keep, north_keep)
        rhs = eta - DIV_K * 0.5 * (east_t[0] - west_t[0] + (north_t[1] - south_t[1]))
        eta = surface_solve(rhs, south_keep, north_keep)
        east_e, west_e, north_e, south_e = surface_sides((eta,), south_keep, north_keep)
        uvel = ocean * (ustar - GRAV_K * 0.5 * (east_e[0] - west_e[0])[:, None])
        vvel = ocean * (vstar - GRAV_K * 0.5 * (north_e[0] - south_e[0])[:, None])
        temp = temp_next
        salt = salt_next
    zonal_scale = 1.0 / jnp.sqrt(jnp.float32(total_cols))
    score_scale = 1.0 / jnp.sqrt(jnp.float32(levels * total_rows))
    lat_weight = latitude / total_rows
    zonal_local = jnp.sum(vvel, axis=3)
    zonal_whole = lax.psum(zonal_local, "gridx")
    overturn = jnp.cumsum(zonal_whole, axis=1) * zonal_scale
    score = lax.psum(jnp.sum(overturn * lat_weight, axis=(1, 2)) * score_scale, "gridy")
    state_stack = jnp.stack((temp, salt, uvel, vvel))
    every_state, every_eta, every_score = (
        lax.all_gather(state_stack, "member", axis=1, tiled=True),
        lax.all_gather(eta, "member", axis=0, tiled=True),
        lax.all_gather(score, "member", axis=0, tiled=True),
    )
    picked = jnp.take(every_state, clone_source, axis=1)
    new_eta = jnp.take(every_eta, clone_source, axis=0)
    clone_weight = jnp.take(every_score, clone_source, axis=0) - jnp.mean(every_score)
    return (picked[0], picked[1], picked[2], picked[3], new_eta, overturn, clone_weight)


def solution(mesh):
    in_specs = (
        P("member", None, "gridy", "gridx"),
        P("member", None, "gridy", "gridx"),
        P("member", None, "gridy", "gridx"),
        P("member", None, "gridy", "gridx"),
        P("member", "gridy", "gridx"),
        P("gridy", "gridx"),
        P("member"),
    )
    out_specs = (
        P("member", None, "gridy", "gridx"),
        P("member", None, "gridy", "gridx"),
        P("member", None, "gridy", "gridx"),
        P("member", None, "gridy", "gridx"),
        P("member", "gridy", "gridx"),
        P("member", None, "gridy"),
        P("member"),
    )
    return jax.shard_map(shards, mesh=mesh, in_specs=in_specs, out_specs=out_specs, check_vma=False)
```

profile of v0, /device:TPU:0, one launch (start us, length us, event | category | flops | bytes accessed | tf_op | source)
XLA Modules:
  0.0 1723.3 jit_solution(7264022242541431259)
XLA Ops:
  25.9 3.5 collective-permute-start.2
  29.5 3.1 pad_maximum_fusion.5
  50.9 4.1 collective-permute-start.6
  64.0 4.1 collective-permute-start.10
  70.7 140.7 %all-reduce.2 = (f32[2]{0:T(128)S(1)}, f32[2]{0:T(128)S(1)}) all-reduce(f32[2]{0:T(128)S(1)} %get-tuple-element.298, f32[2]{0:T(128)S(1)} %get-tuple-element.297), channel_id=1, replica_groups=mesh['member'=2,'gridy'=8,'gridx'=8] {'gridy','gridx'}, use_global_device_ids=true, to_apply=%region_4.5 | all-reduce | flops 4 | bytes 32 | tf_op jit(solution)/shard_map/psum | solution.py:73
  211.6 138.7 %psum.100 = f32[2]{0:T(128)S(1)} all-reduce(f32[2]{0:T(128)S(1)} %get-tuple-element.316), channel_id=1, replica_groups=mesh['member'=2,'gridy'=8,'gridx'=8] {'gridy','gridx'}, use_global_device_ids=true, to_apply=%region_8.9 | all-reduce | flops 2 | bytes 16 | tf_op jit(solution)/shard_map/psum | solution.py:73
  361.6 141.1 %psum.101 = f32[2]{0:T(128)S(1)} all-reduce(f32[2]{0:T(128)S(1)} %get-tuple-element.314), channel_id=1, replica_groups=mesh['member'=2,'gridy'=8,'gridx'=8] {'gridy','gridx'}, use_global_device_ids=true, to_apply=%region_10.11 | all-reduce | flops 2 | bytes 16 | tf_op jit(solution)/shard_map/psum | solution.py:87
  502.8 138.6 %psum.102 = f32[2]{0:T(128)S(1)} all-reduce(f32[2]{0:T(128)S(1)} %multiply_reduce_fusion.5), channel_id=1, replica_groups=mesh['member'=2,'gridy'=8,'gridx'=8] {'gridy','gridx'}, use_global_device_ids=true, to_apply=%region_12.13 | all-reduce | flops 2 | bytes 16 | tf_op jit(solution)/shard_map/psum | solution.py:73
  653.8 3.5 bitcast_dynamic-update-slice_fusion.3
  657.3 141.7 %psum.103 = f32[2]{0:T(128)} all-reduce(f32[2]{0:T(128)} %fusion.143), channel_id=1, replica_groups=mesh['member'=2,'gridy'=8,'gridx'=8] {'gridy','gridx'}, use_global_device_ids=true, to_apply=%region_14.15 | all-reduce | flops 2 | bytes 16 | tf_op jit(solution)/shard_map/psum | solution.py:87
  803.7 3.5 bitcast_dynamic-update-slice_fusion.2
  807.4 4.1 collective-permute-start.22
  820.9 3.0 collective-permute-done.24
  831.4 4.1 collective-permute-start.26
  835.5 3.0 pad_maximum_fusion.3
  849.1 3.4 fusion.175
  852.6 3.0 fusion.173
  860.7 4.1 collective-permute-start.30
  874.9 4.1 collective-permute-start.34
  885.4 139.8 %all-reduce.1 = (f32[2]{0:T(128)}, f32[2]{0:T(128)}) all-reduce(f32[2]{0:T(128)} %get-tuple-element.296, f32[2]{0:T(128)} %get-tuple-element.295), channel_id=1, replica_groups=mesh['member'=2,'gridy'=8,'gridx'=8] {'gridy','gridx'}, use_global_device_ids=true, to_apply=%region_19.20 | all-reduce | flops 4 | bytes 32 | tf_op jit(solution)/shard_map/psum | solution.py:73
  1027.1 140.4 %psum.106 = f32[2]{0:T(128)S(1)} all-reduce(f32[2]{0:T(128)} %get-tuple-element.307), channel_id=1, replica_groups=mesh['member'=2,'gridy'=8,'gridx'=8] {'gridy','gridx'}, use_global_device_ids=true, to_apply=%region_23.24 | all-reduce | flops 2 | bytes 16 | tf_op jit(solution)/shard_map/psum | solution.py:73
  1174.6 3.7 collective-permute-start.38
  1185.3 139.6 %psum.107 = f32[2]{0:T(128)} all-reduce(f32[2]{0:T(128)} %get-tuple-element.305), channel_id=1, replica_groups=mesh['member'=2,'gridy'=8,'gridx'=8] {'gridy','gridx'}, use_global_device_ids=true, to_apply=%region_25.26 | all-reduce | flops 2 | bytes 16 | tf_op jit(solution)/shard_map/psum | solution.py:87
  1327.7 141.5 %psum.108 = f32[2]{0:T(128)} all-reduce(f32[2]{0:T(128)} %multiply_reduce_fusion), channel_id=1, replica_groups=mesh['member'=2,'gridy'=8,'gridx'=8] {'gridy','gridx'}, use_global_device_ids=true, to_apply=%region_27.28 | all-reduce | flops 2 | bytes 16 | tf_op jit(solution)/shard_map/psum | solution.py:73
  1476.2 3.9 collective-permute-start.42
  1486.7 139.5 %psum.109 = f32[2]{0:T(128)} all-reduce(f32[2]{0:T(128)} %fusion.107), channel_id=1, replica_groups=mesh['member'=2,'gridy'=8,'gridx'=8] {'gridy','gridx'}, use_global_device_ids=true, to_apply=%region_29.30 | all-reduce | flops 2 | bytes 16 | tf_op jit(solution)/shard_map/psum | solution.py:87
  1642.6 3.4 fusion.87
  1650.8 20.4 %psum.110 = f32[2,4,64]{2,1,0:T(4,128)S(1)} all-reduce(f32[2,4,64]{2,1,0:T(4,128)S(1)} %copy-done.41), channel_id=1, replica_groups=mesh['member'=2,'gridy'=8,'gridx'=8] {'gridx'}, use_global_device_ids=true, to_apply=%region_31.32 | all-reduce | flops 512 | bytes 4096 | tf_op jit(solution)/shard_map/psum | solution.py:156
  1671.9 9.9 all_gather.10
  1681.8 13.2 psum.111
  1695.8 6.5 all-reduce
  1705.5 6.5 all-gather.2.cloned.1.call-done
  (357 shorter events, 187.2 us)
Async XLA Ops:
  7.2 1704.8 %all-gather.2.cloned.1.call-start = ((), (), s32[]{:S(2)}) async-start(), calls=%async_computation | async-start | bytes 6291456 | tf_op jit(solution)/shard_map/all_gather | solution.py:161
  13.3 4.6 collective-permute-start
  22.4 14.5 collective-permute-start.3
  25.9 12.8 collective-permute-start.2
  46.4 4.3 collective-permute-start.4
  50.8 7.3 collective-permute-start.7
  50.9 7.2 collective-permute-start.6
  64.0 6.5 collective-permute-start.11
  64.0 6.5 collective-permute-start.10
  350.5 4.2 collective-permute-start.12
  354.8 6.5 collective-permute-start.15
  356.9 4.4 collective-permute-start.14
  646.5 6.5 collective-permute-start.19
  648.6 4.4 collective-permute-start.18
  800.7 6.5 collective-permute-start.20
  800.7 6.5 collective-permute-start.21
  807.3 6.5 collective-permute-start.23
  807.4 6.5 collective-permute-start.22
  819.2 4.6 collective-permute-start.24
  828.9 15.3 collective-permute-start.27
  831.4 15.2 collective-permute-start.26
  855.6 4.3 collective-permute-start.28
  860.7 7.8 collective-permute-start.31
  860.7 7.8 collective-permute-start.30
  874.9 8.0 collective-permute-start.35
  874.9 8.7 collective-permute-start.34
  1174.2 8.7 collective-permute-start.39
  1174.6 8.3 collective-permute-start.38
  1476.0 8.7 collective-permute-start.43
  1476.2 8.5 collective-permute-start.42
  1632.2 6.5 collective-permute-start.47
  1634.3 4.4 collective-permute-start.46
  (70 other events, 697.8 us)
Sparse Core Ops, SparseCore 0:
  1649.6 62.2 all-gather.1
where the time goes:
time: 1730 us; the launch traced here: 1720 us
  blocking collectives  1450 us (84%)
  other arithmetic  72.2 us (4%)
  waiting for transfers between devices  61.8 us (4%)
  starting transfers between devices  61.5 us (4%)
  local copies, waits for them, and re-layouts  59.9 us (3%)
    psum x6, blocking collectives, squared_norm(): return lax.psum(member_total(residual * residual), ('gridy', 'gridx'))  840 us
    psum x4, blocking collectives, surface_solve(): lax.psum(member_total(direction * image), ('gridy', 'gridx'))  562 us
    ppermute x24, starting transfers between devices, padded_2(): lax.ppermute(lax.slice_in_dim(block, 0, width, axis=dim), axis, backward)  48 us
    ppermute x24, waiting for transfers between devices, padded_2(): lax.ppermute(lax.slice_in_dim(block, block.shape[dim] - width, None, axis...  45.3 us
  transfers between devices with their start and end apart: 49, of which 29 were waited for; matrix products, arithmetic and copies ran while one was open for 3% of the time, Pallas kernels for 0%

commit v1 on v0

--- a/solution.py
+++ b/solution.py
@@ -34,6 +34,17 @@
     return block
 
 
+def tree_sum(values, axes):
+    for axis in axes:
+        count = lax.axis_size(axis)
+        step = 1
+        while step < count:
+            pairs = [(i, i ^ step) for i in range(count)]
+            values = values + lax.ppermute(values, axis, pairs)
+            step *= 2
+    return values
+
+
 def pressure(temp, salt):
     return PRESS_K * jnp.cumsum(BETA_S * salt - ALPHA_T * temp, axis=-3)
 
@@ -70,7 +81,7 @@
 
 
 def squared_norm(residual):
-    return lax.psum(member_total(residual * residual), ("gridy", "gridx"))
+    return tree_sum(member_total(residual * residual), ("gridy", "gridx"))
 
 
 def widen(values):
@@ -84,7 +95,7 @@
     norm_now = squared_norm(residual)
     for count in range(ITERS):
         image = surface_apply(direction, south_keep, north_keep)
-        alpha = norm_now / lax.psum(member_total(direction * image), ("gridy", "gridx"))
+        alpha = norm_now / tree_sum(member_total(direction * image), ("gridy", "gridx"))
         solution = solution + widen(alpha) * direction
         residual = residual - widen(alpha) * image
         norm_next = squared_norm(residual)
@@ -153,9 +164,9 @@
     score_scale = 1.0 / jnp.sqrt(jnp.float32(levels * total_rows))
     lat_weight = latitude / total_rows
     zonal_local = jnp.sum(vvel, axis=3)
-    zonal_whole = lax.psum(zonal_local, "gridx")
+    zonal_whole = tree_sum(zonal_local, ("gridx",))
     overturn = jnp.cumsum(zonal_whole, axis=1) * zonal_scale
-    score = lax.psum(jnp.sum(overturn * lat_weight, axis=(1, 2)) * score_scale, "gridy")
+    score = tree_sum(jnp.sum(overturn * lat_weight, axis=(1, 2)) * score_scale, ("gridy",))
     state_stack = jnp.stack((temp, salt, uvel, vvel))
     every_state, every_eta, every_score = (
         lax.all_gather(state_stack, "member", axis=1, tiled=True),

time: 1730 us -> 553 us (0.32)
  blocking collectives: 1450 us -> 16.1 us
  waiting for transfers between devices: 61.8 us -> 251 us
  starting transfers between devices: 61.5 us -> 123 us
    psum x12 -> x0, blocking collectives: 1440 us -> none  [the longest x6 840 us: squared_norm(): return lax.psum(member_total(residual * residual), ('gridy', 'gridx'))]
    ppermute x0 -> x78, waiting for transfers between devices: none -> 180 us  [tree_sum(): values = values + lax.ppermute(values, axis, pairs)]
    ppermute x0 -> x78, starting transfers between devices: none -> 61.6 us  [tree_sum(): values = values + lax.ppermute(values, axis, pairs)]
  transfers between devices with their start and end apart: 49 -> 127, of which waited for: 29 -> 101; matrix products, arithmetic and copies ran while one was open for 3% -> 11% of each run, Pallas kernels for 0% -> 0%
where the time goes in v1:
time: 553 us; the launch traced here: 542 us
  waiting for transfers between devices  251 us (45%)
  starting transfers between devices  123 us (22%)
  other arithmetic  72 us (13%)
  local copies, waits for them, and re-layouts  63.5 us (11%)
  between operations  16.7 us (3%)
  blocking collectives  16.1 us (3%)
    ppermute x78, waiting for transfers between devices, tree_sum(): values = values + lax.ppermute(values, axis, pairs)  180 us
    ppermute x78, starting transfers between devices, tree_sum(): values = values + lax.ppermute(values, axis, pairs)  61.6 us
    ppermute x24, starting transfers between devices, padded_2(): lax.ppermute(lax.slice_in_dim(block, 0, width, axis=dim), axis, backward)  50.2 us
    ppermute x24, waiting for transfers between devices, padded_2(): lax.ppermute(lax.slice_in_dim(block, block.shape[dim] - width, None, axis...  40.3 us
    all_gather x1, waiting for transfers between devices, shards(): lax.all_gather(state_stack, 'member', axis=1, tiled=True)  21.4 us
    another operation x12, local copies, waits for them, and re-layouts, split_rims(): south_side = south_side.at[..., 0, :].multiply(south_keep)  13.3 us
    slice x22, local copies, waits for them, and re-layouts, padded_2(): lax.slice_in_dim(block, 0, width, axis=dim)  12.8 us
    another operation x12, local copies, waits for them, and re-layouts, split_rims(): north_side = north_side.at[..., -1, :].multiply(north_keep)  11.5 us
  transfers between devices with their start and end apart: 127, of which 101 were waited for; matrix products, arithmetic and copies ran while one was open for 11% of the time, Pallas kernels for 0%

profile of v1, /device:TPU:0, one launch (start us, length us, event | category | flops | bytes accessed | tf_op | source)
XLA Modules:
  0.0 542.5 jit_solution(18020476195742906736)
XLA Ops:
  25.8 3.5 collective-permute-start.2
  50.8 4.1 collective-permute-start.6
  64.0 4.1 collective-permute-start.16
  129.8 3.5 collective-permute-done.35
  134.0 4.5 collective-permute-done.36
  156.0 4.5 collective-permute-done.42
  173.8 3.6 bitcast_dynamic-update-slice_fusion.3
  189.7 3.5 collective-permute-done.51
  201.8 3.5 collective-permute-done.54
  206.2 4.1 collective-permute-done.55
  218.7 4.1 collective-permute-start.58
  243.2 3.9 collective-permute-start.62
  272.2 4.1 collective-permute-start.66
  286.6 4.1 collective-permute-start.76
  359.7 3.5 collective-permute-done.95
  364.1 4.2 collective-permute-done.96
  376.2 4.2 collective-permute-done.99
  387.7 4.2 collective-permute-done.102
  399.8 4.2 collective-permute-done.105
  411.3 4.1 collective-permute-start.108
  422.6 3.5 collective-permute-done.111
  426.1 5.0 collective-permute-done.112
  431.2 3.5 collective-permute-done.113
  434.7 3.5 collective-permute-done.114
  438.5 4.8 collective-permute-done.115
  449.4 4.1 collective-permute-start.118
  476.2 9.6 %all_gather.10 = f32[4,64,256]{2,1,0:T(8,128)S(1)} all-gather(f32[2,64,256]{2,1,0:T(8,128)S(1)} %copy-done.28), channel_id=1, replica_groups=mesh['member'=2,'gridy'=8,'gridx'=8] {'member'}, dimensions={0}, use_global_device_ids=true | all-gather | bytes 393216 | tf_op jit(solution)/shard_map/all_gather | solution.py:173
  487.6 3.5 collective-permute-done.124
  491.1 5.0 collective-permute-done.125
  496.8 6.5 %all-reduce = f32[4]{0:T(128)S(1)} all-reduce(f32[4]{0:T(128)S(1)} %add_dynamic-update-slice_fusion), channel_id=1, replica_groups=mesh['member'=2,'gridy'=8,'gridx'=8] {'member'}, use_global_device_ids=true, to_apply=%add | all-reduce | flops 4 | bytes 32
  506.5 21.4 %all-gather.2.cloned.1.call-done = f32[4,4,4,64,256]{4,3,2,1,0:T(8,128)} async-done(((f32[4,2,4,64,256]{4,3,2,1,0:T(8,128)}), f32[4,4,4,64,256]{4,3,2,1,0:T(8,128)}) %all-gather.2.cloned.1.call-update) | async-done | bytes 4194320 | tf_op jit(solution)/shard_map/all_gather | solution.py:172
  527.9 4.3 gather_fusion
  (568 shorter events, 370.9 us)
Async XLA Ops:
  7.2 520.7 %all-gather.2.cloned.1.call-start = ((), (), s32[]{:S(2)}) async-start(), calls=%async_computation | async-start | bytes 6291456 | tf_op jit(solution)/shard_map/all_gather | solution.py:172
  22.3 14.5 %collective-permute-start.3 = (f32[5,2,4,66,1]{3,2,4,1,0:T(4,128)S(1)}, f32[5,2,4,66,1]{3,2,4,1,0:T(4,128)S(1)}, u32[]{:S(2)}, u32[]{:S(2)}) collective-permute-start(f32[5,2,4,66,1]{3,2,4,1,0:T(4,128)S(1)} %copy.16), channel_id=1, source_target_pairs={{0,1},{1,2},{2,3},{3,4},{4,5},{5,6},{6,7},{7,0},{8,9},{9,10},{10,1... | collective-permute-start | bytes 31688 | tf_op jit(solution)/shard_map/ppermute | solution.py:29
  25.8 12.7 %collective-permute-start.2 = (f32[5,2,4,66,1]{3,2,4,1,0:T(4,128)S(1)}, f32[5,2,4,66,1]{3,2,4,1,0:T(4,128)S(1)}, u32[]{:S(2)}, u32[]{:S(2)}) collective-permute-start(f32[5,2,4,66,1]{3,2,4,1,0:T(4,128)S(1)} %copy.14), channel_id=1, source_target_pairs={{1,0},{2,1},{3,2},{4,3},{5,4},{6,5},{7,6},{0,7},{9,8},{10,9},{11,1... | collective-permute-start | bytes 31688 | tf_op jit(solution)/shard_map/ppermute | solution.py:32
  50.7 7.3 %collective-permute-start.7 = (f32[2,2,66,1]{3,2,1,0:T(8,128)S(1)}, f32[2,2,66,1]{3,2,1,0:T(8,128)S(1)}, u32[]{:S(2)}, u32[]{:S(2)}) collective-permute-start(f32[2,2,66,1]{3,2,1,0:T(8,128)S(1)} %get-tuple-element.356), channel_id=1, source_target_pairs={{0,1},{1,2},{2,3},{3,4},{4,5},{5,6},{6,7},{7,0},{8,9},{9,10},{10,1... | collective-permute-start | bytes 3176 | tf_op jit(solution)/shard_map/ppermute | solution.py:29
  50.8 7.2 %collective-permute-start.6 = (f32[2,2,66,1]{3,2,1,0:T(8,128)S(1)}, f32[2,2,66,1]{3,2,1,0:T(8,128)S(1)}, u32[]{:S(2)}, u32[]{:S(2)}) collective-permute-start(f32[2,2,66,1]{3,2,1,0:T(8,128)S(1)} %get-tuple-element.355), channel_id=1, source_target_pairs={{1,0},{2,1},{3,2},{4,3},{5,4},{6,5},{7,6},{0,7},{9,8},{10,9},{11,1... | collective-permute-start | bytes 3176 | tf_op jit(solution)/shard_map/ppermute | solution.py:32
  63.9 6.5 %collective-permute-start.17 = (f32[1,2,66,1]{3,2,1,0:T(8,128)S(1)}, f32[1,2,66,1]{3,2,1,0:T(8,128)S(1)}, u32[]{:S(2)}, u32[]{:S(2)}) collective-permute-start(f32[1,2,66,1]{3,2,1,0:T(8,128)S(1)} %get-tuple-element.380), channel_id=1, source_target_pairs={{0,1},{1,2},{2,3},{3,4},{4,5},{5,6},{6,7},{7,0},{8,9},{9,10},{10,1... | collective-permute-start | bytes 1592 | tf_op jit(solution)/shard_map/ppermute | solution.py:29
  64.0 6.5 %collective-permute-start.16 = (f32[1,2,66,1]{3,2,1,0:T(8,128)S(1)}, f32[1,2,66,1]{3,2,1,0:T(8,128)S(1)}, u32[]{:S(2)}, u32[]{:S(2)}) collective-permute-start(f32[1,2,66,1]{3,2,1,0:T(8,128)S(1)} %get-tuple-element.379), channel_id=1, source_target_pairs={{1,0},{2,1},{3,2},{4,3},{5,4},{6,5},{7,6},{0,7},{9,8},{10,9},{11,1... | collective-permute-start | bytes 1592 | tf_op jit(solution)/shard_map/ppermute | solution.py:32
  75.4 5.0 collective-permute-start.20
  75.6 6.3 %collective-permute-start.10 = (f32[2]{0:T(128)S(1)}, f32[2]{0:T(128)S(1)}, u32[]{:S(2)}, u32[]{:S(2)}) collective-permute-start(f32[2]{0:T(128)S(1)} %add.616), channel_id=1, source_target_pairs={{0,32},{8,40},{16,48},{24,56},{32,0},{40,8},{48,16},{56,24},{1,33}... | collective-permute-start | bytes 32 | tf_op jit(solution)/shard_map/ppermute | solution.py:43
  90.2 5.0 collective-permute-start.13
  121.9 6.5 %collective-permute-start.33 = (f32[1,2,66,1]{3,2,1,0:T(8,128)S(1)}, f32[1,2,66,1]{3,2,1,0:T(8,128)S(1)}, u32[]{:S(2)}, u32[]{:S(2)}) collective-permute-start(f32[1,2,66,1]{3,2,1,0:T(8,128)S(1)} %get-tuple-element.378), channel_id=1, source_target_pairs={{0,1},{1,2},{2,3},{3,4},{4,5},{5,6},{6,7},{7,0},{8,9},{9,10},{10,1... | collective-permute-start | bytes 1592 | tf_op jit(solution)/shard_map/ppermute | solution.py:29
  178.3 8.7 %collective-permute-start.49 = (f32[1,2,66,1]{3,2,1,0:T(8,128)}, f32[1,2,66,1]{3,2,1,0:T(8,128)}, u32[]{:S(2)}, u32[]{:S(2)}) collective-permute-start(f32[1,2,66,1]{3,2,1,0:T(8,128)} %get-tuple-element.376), channel_id=1, source_target_pairs={{0,1},{1,2},{2,3},{3,4},{4,5},{5,6},{6,7},{7,0},{8,9},{9,10},{10,1... | collective-permute-start | bytes 1592 | tf_op jit(solution)/shard_map/ppermute | solution.py:29
  179.4 7.6 %collective-permute-start.48 = (f32[1,2,66,1]{3,2,1,0:T(8,128)}, f32[1,2,66,1]{3,2,1,0:T(8,128)}, u32[]{:S(2)}, u32[]{:S(2)}) collective-permute-start(f32[1,2,66,1]{3,2,1,0:T(8,128)} %get-tuple-element.375), channel_id=1, source_target_pairs={{1,0},{2,1},{3,2},{4,3},{5,4},{6,5},{7,6},{0,7},{9,8},{10,9},{11,1... | collective-permute-start | bytes 1592 | tf_op jit(solution)/shard_map/ppermute | solution.py:32
  212.0 6.5 %collective-permute-start.56 = (f32[1,2,1,256]{3,2,1,0:T(1,128)S(1)}, f32[1,2,1,256]{3,2,1,0:T(1,128)S(1)}, u32[]{:S(2)}, u32[]{:S(2)}) collective-permute-start(f32[1,2,1,256]{3,2,1,0:T(1,128)S(1)} %get-tuple-element.401), channel_id=1, source_target_pairs={{0,8},{8,16},{16,24},{24,32},{32,40},{40,48},{48,56},{56,0},{1,9},... | collective-permute-start | bytes 6152 | tf_op jit(solution)/shard_map/ppermute | solution.py:29
  212.1 6.5 %collective-permute-start.57 = (f32[1,2,1,256]{3,2,1,0:T(1,128)S(1)}, f32[1,2,1,256]{3,2,1,0:T(1,128)S(1)}, u32[]{:S(2)}, u32[]{:S(2)}) collective-permute-start(f32[1,2,1,256]{3,2,1,0:T(1,128)S(1)} %get-tuple-element.402), channel_id=1, source_target_pairs={{8,0},{16,8},{24,16},{32,24},{40,32},{48,40},{56,48},{0,56},{9,1},... | collective-permute-start | bytes 6152 | tf_op jit(solution)/shard_map/ppermute | solution.py:32
  218.6 6.5 %collective-permute-start.59 = (f32[1,2,66,1]{3,2,1,0:T(8,128)S(1)}, f32[1,2,66,1]{3,2,1,0:T(8,128)S(1)}, u32[]{:S(2)}, u32[]{:S(2)}) collective-permute-start(f32[1,2,66,1]{3,2,1,0:T(8,128)S(1)} %get-tuple-element.374), channel_id=1, source_target_pairs={{0,1},{1,2},{2,3},{3,4},{4,5},{5,6},{6,7},{7,0},{8,9},{9,10},{10,1... | collective-permute-start | bytes 1592 | tf_op jit(solution)/shard_map/ppermute | solution.py:29
  218.7 6.5 %collective-permute-start.58 = (f32[1,2,66,1]{3,2,1,0:T(8,128)S(1)}, f32[1,2,66,1]{3,2,1,0:T(8,128)S(1)}, u32[]{:S(2)}, u32[]{:S(2)}) collective-permute-start(f32[1,2,66,1]{3,2,1,0:T(8,128)S(1)} %get-tuple-element.373), channel_id=1, source_target_pairs={{1,0},{2,1},{3,2},{4,3},{5,4},{6,5},{7,6},{0,7},{9,8},{10,9},{11,1... | collective-permute-start | bytes 1592 | tf_op jit(solution)/shard_map/ppermute | solution.py:32
  240.4 15.3 %collective-permute-start.63 = (f32[5,2,4,66,1]{3,2,4,1,0:T(4,128)}, f32[5,2,4,66,1]{3,2,4,1,0:T(4,128)}, u32[]{:S(2)}, u32[]{:S(2)}) collective-permute-start(f32[5,2,4,66,1]{3,2,4,1,0:T(4,128)} %copy.20), channel_id=1, source_target_pairs={{0,1},{1,2},{2,3},{3,4},{4,5},{5,6},{6,7},{7,0},{8,9},{9,10},{10,1... | collective-permute-start | bytes 31688 | tf_op jit(solution)/shard_map/ppermute | solution.py:29
  243.2 15.1 %collective-permute-start.62 = (f32[5,2,4,66,1]{3,2,4,1,0:T(4,128)}, f32[5,2,4,66,1]{3,2,4,1,0:T(4,128)}, u32[]{:S(2)}, u32[]{:S(2)}) collective-permute-start(f32[5,2,4,66,1]{3,2,4,1,0:T(4,128)} %copy.18), channel_id=1, source_target_pairs={{1,0},{2,1},{3,2},{4,3},{5,4},{6,5},{7,6},{0,7},{9,8},{10,9},{11,1... | collective-permute-start | bytes 31688 | tf_op jit(solution)/shard_map/ppermute | solution.py:32
  272.2 7.8 %collective-permute-start.67 = (f32[2,2,66,1]{3,2,1,0:T(8,128)}, f32[2,2,66,1]{3,2,1,0:T(8,128)}, u32[]{:S(2)}, u32[]{:S(2)}) collective-permute-start(f32[2,2,66,1]{3,2,1,0:T(8,128)} %get-tuple-element.354), channel_id=1, source_target_pairs={{0,1},{1,2},{2,3},{3,4},{4,5},{5,6},{6,7},{7,0},{8,9},{9,10},{10,1... | collective-permute-start | bytes 3176 | tf_op jit(solution)/shard_map/ppermute | solution.py:29
  272.2 7.8 %collective-permute-start.66 = (f32[2,2,66,1]{3,2,1,0:T(8,128)}, f32[2,2,66,1]{3,2,1,0:T(8,128)}, u32[]{:S(2)}, u32[]{:S(2)}) collective-permute-start(f32[2,2,66,1]{3,2,1,0:T(8,128)} %get-tuple-element.353), channel_id=1, source_target_pairs={{1,0},{2,1},{3,2},{4,3},{5,4},{6,5},{7,6},{0,7},{9,8},{10,9},{11,1... | collective-permute-start | bytes 3176 | tf_op jit(solution)/shard_map/ppermute | solution.py:32
  286.6 8.0 %collective-permute-start.77 = (f32[1,2,66,1]{3,2,1,0:T(8,128)}, f32[1,2,66,1]{3,2,1,0:T(8,128)}, u32[]{:S(2)}, u32[]{:S(2)}) collective-permute-start(f32[1,2,66,1]{3,2,1,0:T(8,128)} %get-tuple-element.372), channel_id=1, source_target_pairs={{0,1},{1,2},{2,3},{3,4},{4,5},{5,6},{6,7},{7,0},{8,9},{9,10},{10,1... | collective-permute-start | bytes 1592 | tf_op jit(solution)/shard_map/ppermute | solution.py:29
  286.6 8.7 %collective-permute-start.76 = (f32[1,2,66,1]{3,2,1,0:T(8,128)}, f32[1,2,66,1]{3,2,1,0:T(8,128)}, u32[]{:S(2)}, u32[]{:S(2)}) collective-permute-start(f32[1,2,66,1]{3,2,1,0:T(8,128)} %get-tuple-element.371), channel_id=1, source_target_pairs={{1,0},{2,1},{3,2},{4,3},{5,4},{6,5},{7,6},{0,7},{9,8},{10,9},{11,1... | collective-permute-start | bytes 1592 | tf_op jit(solution)/shard_map/ppermute | solution.py:32
  310.1 5.3 collective-permute-start.72
  315.4 5.0 collective-permute-start.73
  348.6 8.7 %collective-permute-start.93 = (f32[1,2,66,1]{3,2,1,0:T(8,128)}, f32[1,2,66,1]{3,2,1,0:T(8,128)}, u32[]{:S(2)}, u32[]{:S(2)}) collective-permute-start(f32[1,2,66,1]{3,2,1,0:T(8,128)} %get-tuple-element.370), channel_id=1, source_target_pairs={{0,1},{1,2},{2,3},{3,4},{4,5},{5,6},{6,7},{7,0},{8,9},{9,10},{10,1... | collective-permute-start | bytes 1592 | tf_op jit(solution)/shard_map/ppermute | solution.py:29
  350.2 7.1 %collective-permute-start.92 = (f32[1,2,66,1]{3,2,1,0:T(8,128)}, f32[1,2,66,1]{3,2,1,0:T(8,128)}, u32[]{:S(2)}, u32[]{:S(2)}) collective-permute-start(f32[1,2,66,1]{3,2,1,0:T(8,128)} %get-tuple-element.369), channel_id=1, source_target_pairs={{1,0},{2,1},{3,2},{4,3},{5,4},{6,5},{7,6},{0,7},{9,8},{10,9},{11,1... | collective-permute-start | bytes 1592 | tf_op jit(solution)/shard_map/ppermute | solution.py:32
  411.3 8.7 %collective-permute-start.109 = (f32[1,2,66,1]{3,2,1,0:T(8,128)}, f32[1,2,66,1]{3,2,1,0:T(8,128)}, u32[]{:S(2)}, u32[]{:S(2)}) collective-permute-start(f32[1,2,66,1]{3,2,1,0:T(8,128)} %get-tuple-element.368), channel_id=1, source_target_pairs={{0,1},{1,2},{2,3},{3,4},{4,5},{5,6},{6,7},{7,0},{8,9},{9,10},{10,1... | collective-permute-start | bytes 1592 | tf_op jit(solution)/shard_map/ppermute | solution.py:29
  411.3 8.7 %collective-permute-start.108 = (f32[1,2,66,1]{3,2,1,0:T(8,128)}, f32[1,2,66,1]{3,2,1,0:T(8,128)}, u32[]{:S(2)}, u32[]{:S(2)}) collective-permute-start(f32[1,2,66,1]{3,2,1,0:T(8,128)} %get-tuple-element.367), channel_id=1, source_target_pairs={{1,0},{2,1},{3,2},{4,3},{5,4},{6,5},{7,6},{0,7},{9,8},{10,9},{11,1... | collective-permute-start | bytes 1592 | tf_op jit(solution)/shard_map/ppermute | solution.py:32
  449.4 6.5 %collective-permute-start.119 = (f32[1,2,66,1]{3,2,1,0:T(8,128)S(1)}, f32[1,2,66,1]{3,2,1,0:T(8,128)S(1)}, u32[]{:S(2)}, u32[]{:S(2)}) collective-permute-start(f32[1,2,66,1]{3,2,1,0:T(8,128)S(1)} %get-tuple-element.366), channel_id=1, source_target_pairs={{0,1},{1,2},{2,3},{3,4},{4,5},{5,6},{6,7},{7,0},{8,9},{9,10},{10,1... | collective-permute-start | bytes 1592 | tf_op jit(solution)/shard_map/ppermute | solution.py:29
  449.4 6.5 %collective-permute-start.118 = (f32[1,2,66,1]{3,2,1,0:T(8,128)S(1)}, f32[1,2,66,1]{3,2,1,0:T(8,128)S(1)}, u32[]{:S(2)}, u32[]{:S(2)}) collective-permute-start(f32[1,2,66,1]{3,2,1,0:T(8,128)S(1)} %get-tuple-element.365), channel_id=1, source_target_pairs={{1,0},{2,1},{3,2},{4,3},{5,4},{6,5},{7,6},{0,7},{9,8},{10,9},{11,1... | collective-permute-start | bytes 1592 | tf_op jit(solution)/shard_map/ppermute | solution.py:32
  474.1 11.7 %collective-permute-start.122 = (f32[2,4,64]{2,1,0:T(4,128)S(1)}, f32[2,4,64]{2,1,0:T(4,128)S(1)}, u32[]{:S(2)}, u32[]{:S(2)}) collective-permute-start(f32[2,4,64]{2,1,0:T(4,128)S(1)} %add.751), channel_id=1, source_target_pairs={{0,4},{1,5},{2,6},{3,7},{4,0},{5,1},{6,2},{7,3},{8,12},{9,13},{10,... | collective-permute-start | bytes 6152 | tf_op jit(solution)/shard_map/ppermute | solution.py:43
  (149 other events, 821.3 us)
Sparse Core Ops, SparseCore 0:
  466.7 61.1 all-gather.1
